TPU v7x, 256 devices: a whole 4x4x8 slice. The times are simulated.
256 devices in a mesh: blk: 8 (over x, core), sub: 32 (over z, y).
Axes of the slice: x: 4, y: 4, z: 8, core: 2. Of those that a mesh axis runs over, the one named last changes fastest.
Arguments:
- user_factors: float32 [262144, 1024], P(('blk', 'sub')), may hold values from -6 to 6
- item_factors: bfloat16 [2048, 1024], P(('blk', 'sub')), may hold values from -6 to 6
- ratings: bfloat16 [262144, 1024], P(('blk', 'sub')), may hold values from -6 to 6
- presence: int32 [2048, 8, 2], P(('blk', 'sub')), may hold values 0 or 1
- visit_order: int32 [8], replicated, may hold values from 0 to 7, each once
Outputs:
- users_out: float32 [262144, 1024], P(('blk', 'sub'))
- items_out: bfloat16 [2048, 1024], P(('blk', 'sub'))
All inputs are finite; a program needn't handle non-finite values. No bound on the sum of `presence` on one device may be relied on, other than what follows from the above.
Results may differ from a plain program's by a relative error of at most 0.017.
Values may be sent and summed in bfloat16 or wider, within the bound.
No kernel may reach another device: no remote copies, remote signals or barrier semaphores. Data moves between devices by JAX's collectives and lax.ppermute only.
A program may use at most 64 MiB of HBM per device.

v0:
```python
import math
import jax
import jax.numpy as jnp
from jax import lax
from jax.sharding import PartitionSpec as P

R = 1024
BS = 256
TICKS = 4
learn_users = 0.5
decay_weight = 0.05


def passed_along(block, axis, distance):
    devices = range(lax.axis_size(axis))
    route = [((i - distance) % len(devices), i) for i in devices]
    return lax.ppermute(block, axis, route)


def on_device(user_factors, item_factors, ratings, presence, visit_order):
    scale = R ** (-0.5)
    group_count = lax.axis_size("blk")
    group = lax.axis_index("blk")
    part_index = lax.axis_index("sub")
    part_rows = item_factors.shape[0]
    local_users = user_factors.shape[0]
    group_users = lax.axis_size("sub") * local_users
    step_items = 0.9 * R / (math.sqrt(group_users) + math.sqrt(R)) ** 2
    tile_users = presence.shape[0]
    tile_items = presence.shape[2]
    users_now = user_factors
    item_block = lax.all_gather(item_factors, "sub", axis=0, tiled=True)
    for step_index in range(TICKS):
        position = jnp.mod(group - step_index, group_count)
        ident = jnp.sum(jnp.where(jnp.arange(group_count) == position, visit_order, 0))
        picked = lax.dynamic_index_in_dim(presence, ident, 1, keepdims=False)
        present = jnp.broadcast_to(
            picked[:, None, :, None],
            (tile_users, local_users // tile_users, tile_items, BS // tile_items),
        )
        present = present.reshape(local_users, BS).astype(jnp.float32)
        users_half = users_now.astype(jnp.bfloat16)
        predicted = (
            lax.dot_general(
                users_half, item_block, (((1,), (1,)), ((), ())), preferred_element_type=jnp.float32
            )
            * scale
        )
        targets = ratings[:, step_index * BS : (step_index + 1) * BS].astype(jnp.float32)
        residual = (present * (predicted - targets)).astype(jnp.bfloat16)
        user_grad = jnp.dot(residual, item_block, preferred_element_type=jnp.float32) * scale
        item_part = (
            lax.dot_general(
                residual, users_half, (((0,), (0,)), ((), ())), preferred_element_type=jnp.float32
            )
            * scale
        ).astype(jnp.bfloat16)
        users_now = users_now - learn_users * (user_grad + decay_weight * users_now)
        item_grad = lax.psum(item_part, "sub").astype(jnp.float32)
        block_wide = item_block.astype(jnp.float32)
        updated = (block_wide - step_items * (item_grad + decay_weight * block_wide)).astype(
            jnp.bfloat16
        )
        item_block = passed_along(updated, "blk", 1)
    held_part = lax.dynamic_slice_in_dim(item_block, part_index * part_rows, part_rows, 0)
    return (users_now, held_part)


def solution(mesh):
    in_specs = (
        P(("blk", "sub"), None),
        P(("blk", "sub"), None),
        P(("blk", "sub"), None),
        P(("blk", "sub"), None, None),
        P(),
    )
    out_specs = (P(("blk", "sub"), None), P(("blk", "sub"), None))
    return jax.shard_map(
        on_device, mesh=mesh, in_specs=in_specs, out_specs=out_specs, check_vma=False
    )
```

profile of v0, /device:TPU:1, one launch (start us, length us, event | category | flops | bytes accessed | tf_op | source)
XLA Modules:
  0.0 718.2 jit_solution(10500018908168411886)
XLA Ops:
  7.3 1.4 fusion.39
  16.3 0.9 constant_dynamic-slice_fusion.1
  17.5 42.6 %all_gather.3 = bf16[256,1024]{1,0:T(8,128)(2,1)S(1)} all-gather(bf16[8,1024]{1,0:T(8,128)(2,1)} %param.6), channel_id=1, replica_groups=mesh['blk'=8,'sub'=32] {'sub'}, dimensions={0}, use_global_device_ids=true | all-gather | bytes 540672 | tf_op jit(solution)/shard_map/all_gather | solution.py:32
  60.4 3.1 fusion.8
  63.5 1.5 fusion.9
  65.2 153.3 %all-reduce.5.cloned.1.call-done = bf16[256,1024]{1,0:T(8,128)(2,1)} async-done(((bf16[256,1024]{1,0:T(8,128)(2,1)}), bf16[256,1024]{1,0:T(8,128)(2,1)}) %all-reduce.5.cloned.1.call-update) | async-done | bytes 524304 | tf_op jit(solution)/shard_map/psum | solution.py:59
  218.5 1.3 fusion.18
  219.8 6.3 collective-permute-start
  226.1 3.1 multiply_subtract_fusion.3
  229.2 2.9 collective-permute-done
  232.5 1.8 fusion.10
  234.3 1.6 fusion.11
  236.0 142.1 %all-reduce.7.cloned.1.call-done = bf16[256,1024]{1,0:T(8,128)(2,1)} async-done(((bf16[256,1024]{1,0:T(8,128)(2,1)}), bf16[256,1024]{1,0:T(8,128)(2,1)}) %all-reduce.7.cloned.1.call-update) | async-done | bytes 524304 | tf_op jit(solution)/shard_map/psum | solution.py:59
  378.1 1.3 fusion.21
  379.4 6.3 collective-permute-start.1
  385.8 3.1 multiply_subtract_fusion.2
  388.9 2.9 collective-permute-done.1
  392.1 1.8 fusion.12
  394.0 1.5 fusion.13
  395.9 141.9 %all-reduce.9.cloned.1.call-done = bf16[256,1024]{1,0:T(8,128)(2,1)} async-done(((bf16[256,1024]{1,0:T(8,128)(2,1)}), bf16[256,1024]{1,0:T(8,128)(2,1)}) %all-reduce.9.cloned.1.call-update) | async-done | bytes 524304 | tf_op jit(solution)/shard_map/psum | solution.py:59
  537.8 1.3 fusion.24
  539.0 6.3 collective-permute-start.2
  545.4 3.1 multiply_subtract_fusion.1
  548.5 2.9 collective-permute-done.2
  551.8 1.8 fusion.14
  553.6 1.6 fusion.15
  555.2 142.3 %all-reduce.11.cloned.1.call-done = bf16[256,1024]{1,0:T(8,128)(2,1)} async-done(((bf16[256,1024]{1,0:T(8,128)(2,1)}), bf16[256,1024]{1,0:T(8,128)(2,1)}) %all-reduce.11.cloned.1.call-update) | async-done | bytes 524304 | tf_op jit(solution)/shard_map/psum | solution.py:59
  697.4 1.3 fusion.27
  698.7 6.3 collective-permute-start.3
  705.0 5.1 multiply_subtract_fusion
  710.1 1.0 collective-permute-done.3
  711.1 0.6 constant_dynamic-slice_fusion
  (32 shorter events, 2.5 us)
Async XLA Ops:
  7.2 211.3 %all-reduce.5.cloned.1.call-start = ((), (), s32[]{:S(2)}) async-start(), calls=%async_computation | async-start | bytes 1048576 | tf_op jit(solution)/shard_map/psum | solution.py:59
  17.4 46.0 %copy-start.3 = (f32[1024,1024]{1,0:T(8,128)S(1)}, f32[1024,1024]{1,0:T(8,128)}, u32[]{:S(2)}) copy-start(f32[1024,1024]{1,0:T(8,128)} %param.5) | copy-start | bytes 12582916
  65.0 313.1 %all-reduce.7.cloned.1.call-start = ((), (), s32[]{:S(2)}) async-start(), calls=%async_computation.1 | async-start | bytes 1048576 | tf_op jit(solution)/shard_map/psum | solution.py:59
  219.8 12.4 %collective-permute-start = (bf16[256,1024]{1,0:T(8,128)(2,1)S(1)}, bf16[256,1024]{1,0:T(8,128)(2,1)S(1)}, u32[]{:S(2)}, u32[]{:S(2)}) collective-permute-start(bf16[256,1024]{1,0:T(8,128)(2,1)S(1)} %fusion.18), channel_id=1, source_target_pairs={{224,0},{0,32},{32,64},{64,96},{96,128},{128,160},{160,192},{192,2... | collective-permute-start | bytes 1572872 | tf_op jit(solution)/shard_map/ppermute | solution.py:17
  229.2 5.1 copy-start.2
  235.9 301.9 %all-reduce.9.cloned.1.call-start = ((), (), s32[]{:S(2)}) async-start(), calls=%async_computation.2 | async-start | bytes 1048576 | tf_op jit(solution)/shard_map/psum | solution.py:59
  379.4 12.4 %collective-permute-start.1 = (bf16[256,1024]{1,0:T(8,128)(2,1)S(1)}, bf16[256,1024]{1,0:T(8,128)(2,1)S(1)}, u32[]{:S(2)}, u32[]{:S(2)}) collective-permute-start(bf16[256,1024]{1,0:T(8,128)(2,1)S(1)} %fusion.21), channel_id=1, source_target_pairs={{224,0},{0,32},{32,64},{64,96},{96,128},{128,160},{160,192},{192,2... | collective-permute-start | bytes 1572872 | tf_op jit(solution)/shard_map/ppermute | solution.py:17
  388.9 5.1 copy-start.1
  395.6 301.9 %all-reduce.11.cloned.1.call-start = ((), (), s32[]{:S(2)}) async-start(), calls=%async_computation.3 | async-start | bytes 1048576 | tf_op jit(solution)/shard_map/psum | solution.py:59
  539.0 12.4 %collective-permute-start.2 = (bf16[256,1024]{1,0:T(8,128)(2,1)S(1)}, bf16[256,1024]{1,0:T(8,128)(2,1)S(1)}, u32[]{:S(2)}, u32[]{:S(2)}) collective-permute-start(bf16[256,1024]{1,0:T(8,128)(2,1)S(1)} %fusion.24), channel_id=1, source_target_pairs={{224,0},{0,32},{32,64},{64,96},{96,128},{128,160},{160,192},{192,2... | collective-permute-start | bytes 1572872 | tf_op jit(solution)/shard_map/ppermute | solution.py:17
  548.5 5.1 copy-start
  698.7 12.4 %collective-permute-start.3 = (bf16[256,1024]{1,0:T(8,128)(2,1)S(1)}, bf16[256,1024]{1,0:T(8,128)(2,1)S(1)}, u32[]{:S(2)}, u32[]{:S(2)}) collective-permute-start(bf16[256,1024]{1,0:T(8,128)(2,1)S(1)} %fusion.27), channel_id=1, source_target_pairs={{224,0},{0,32},{32,64},{64,96},{96,128},{128,160},{160,192},{192,2... | collective-permute-start | bytes 1572872 | tf_op jit(solution)/shard_map/ppermute | solution.py:17
Sparse Core Ops, SparseCore 0:
  65.2 153.2 all-reduce.4
  236.0 142.0 all-reduce.6
  395.7 142.0 all-reduce.8
  555.3 142.0 all-reduce.10
where the time goes:
time: 719 us; the launch traced here: 718 us
  waiting for transfers between devices  589 us (82%)
  blocking collectives  42.6 us (6%)
  matrix products  29.2 us (4%)
  starting transfers between devices  25.4 us (4%)
  between operations  21.6 us (3%)
    psum x4, waiting for transfers between devices, on_device(): item_grad = lax.psum(item_part, 'sub').astype(jnp.float32)  580 us
    all_gather x1, blocking collectives, on_device(): item_block = lax.all_gather(item_factors, 'sub', axis=0, tiled=True)  42.6 us
    ppermute x4, starting transfers between devices, passed_along(): return lax.ppermute(block, axis, route)  25 us
    dot_general x4, matrix products, on_device(): jnp.dot(residual, item_block, preferred_element_type=jnp.float32) * scale  14.4 us
  transfers between devices with their start and end apart: 8, of which 8 were waited for; matrix products, arithmetic and copies ran while one was open for 2% of the time, Pallas kernels for 0%

commit v1 on v0

--- a/solution.py
+++ b/solution.py
@@ -29,7 +29,8 @@
     tile_users = presence.shape[0]
     tile_items = presence.shape[2]
     users_now = user_factors
-    item_block = lax.all_gather(item_factors, "sub", axis=0, tiled=True)
+    sent = jnp.stack([item_factors] * lax.axis_size("sub"))
+    item_block = jnp.concatenate(lax.all_to_all(sent, "sub", 0, 0), axis=0)
     for step_index in range(TICKS):
         position = jnp.mod(group - step_index, group_count)
         ident = jnp.sum(jnp.where(jnp.arange(group_count) == position, visit_order, 0))

time: 719 us -> 685 us (0.953)
  blocking collectives: 42.6 us -> 0 us
  starting transfers between devices: 25.4 us -> 37.4 us
    all_gather x1 -> x0, blocking collectives: 42.6 us -> none  [on_device(): item_block = lax.all_gather(item_factors, 'sub', axis=0, tiled=True)]
    all_to_all x0 -> x1, starting transfers between devices: none -> 12 us  [on_device(): item_block = jnp.concatenate(lax.all_to_all(sent, 'sub', 0, 0), axis=0)]
    psum x4, waiting for transfers between devices: 580 us -> 569 us  [on_device(): item_grad = lax.psum(item_part, 'sub').astype(jnp.float32)]
  transfers between devices with their start and end apart: 8 -> 9, of which waited for: 8 -> 9; matrix products, arithmetic and copies ran while one was open for 2% -> 3% of each run, Pallas kernels for 0% -> 0%
where the time goes in v1:
time: 685 us; the launch traced here: 684 us
  waiting for transfers between devices  585 us (85%)
  starting transfers between devices  37.4 us (5%)
  matrix products  29.4 us (4%)
  between operations  21.4 us (3%)
    psum x4, waiting for transfers between devices, on_device(): item_grad = lax.psum(item_part, 'sub').astype(jnp.float32)  569 us
    ppermute x4, starting transfers between devices, passed_along(): return lax.ppermute(block, axis, route)  25 us
    dot_general x4, matrix products, on_device(): jnp.dot(residual, item_block, preferred_element_type=jnp.float32) * scale  14.4 us
  transfers between devices with their start and end apart: 9, of which 9 were waited for; matrix products, arithmetic and copies ran while one was open for 3% of the time, Pallas kernels for 0%

profile of v1, /device:TPU:1, one launch (start us, length us, event | category | flops | bytes accessed | tf_op | source)
XLA Modules:
  0.0 684.4 jit_solution(2204255272230044404)
XLA Ops:
  7.2 1.6 stack.2
  8.7 12.0 %all-to-all-start = ((bf16[32,8,1024]{2,1,0:T(8,128)(2,1)}), bf16[32,8,1024]{2,1,0:T(8,128)(2,1)S(1)}, u32[]{:S(2)}, u32[]{:S(2)}) async-start(bf16[32,8,1024]{2,1,0:T(8,128)(2,1)} %stack.2), calls=%async_computation | async-start | bytes 1048576 | tf_op jit(solution)/shard_map/all_to_all | solution.py:33
  20.9 1.4 fusion.41
  30.8 6.2 all-to-all-done
  37.4 3.2 fusion.8
  40.7 1.5 fusion.9
  42.4 142.2 %all-reduce.5.cloned.1.call-done = bf16[256,1024]{1,0:T(8,128)(2,1)} async-done(((bf16[256,1024]{1,0:T(8,128)(2,1)}), bf16[256,1024]{1,0:T(8,128)(2,1)}) %all-reduce.5.cloned.1.call-update) | async-done | bytes 524304 | tf_op jit(solution)/shard_map/psum | solution.py:60
  184.6 1.3 fusion.18
  185.9 6.3 collective-permute-start
  192.2 3.1 multiply_subtract_fusion.3
  195.3 2.9 collective-permute-done
  198.6 1.8 fusion.10
  200.5 1.6 fusion.11
  202.2 142.1 %all-reduce.7.cloned.1.call-done = bf16[256,1024]{1,0:T(8,128)(2,1)} async-done(((bf16[256,1024]{1,0:T(8,128)(2,1)}), bf16[256,1024]{1,0:T(8,128)(2,1)}) %all-reduce.7.cloned.1.call-update) | async-done | bytes 524304 | tf_op jit(solution)/shard_map/psum | solution.py:60
  344.3 1.3 fusion.21
  345.5 6.3 collective-permute-start.1
  351.9 3.1 multiply_subtract_fusion.2
  355.0 2.9 collective-permute-done.1
  358.3 1.8 fusion.12
  360.1 1.5 fusion.13
  362.0 142.0 %all-reduce.9.cloned.1.call-done = bf16[256,1024]{1,0:T(8,128)(2,1)} async-done(((bf16[256,1024]{1,0:T(8,128)(2,1)}), bf16[256,1024]{1,0:T(8,128)(2,1)}) %all-reduce.9.cloned.1.call-update) | async-done | bytes 524304 | tf_op jit(solution)/shard_map/psum | solution.py:60
  504.0 1.3 fusion.24
  505.3 6.3 collective-permute-start.2
  511.6 3.1 multiply_subtract_fusion.1
  514.7 2.9 collective-permute-done.2
  518.0 1.8 fusion.14
  519.8 1.6 fusion.15
  521.4 142.2 %all-reduce.11.cloned.1.call-done = bf16[256,1024]{1,0:T(8,128)(2,1)} async-done(((bf16[256,1024]{1,0:T(8,128)(2,1)}), bf16[256,1024]{1,0:T(8,128)(2,1)}) %all-reduce.11.cloned.1.call-update) | async-done | bytes 524304 | tf_op jit(solution)/shard_map/psum | solution.py:60
  663.6 1.3 fusion.27
  664.9 6.3 collective-permute-start.3
  671.2 5.1 multiply_subtract_fusion
  676.3 1.0 collective-permute-done.3
  (34 shorter events, 4.1 us)
Async XLA Ops:
  8.7 28.3 %all-to-all-start = ((bf16[32,8,1024]{2,1,0:T(8,128)(2,1)}), bf16[32,8,1024]{2,1,0:T(8,128)(2,1)S(1)}, u32[]{:S(2)}, u32[]{:S(2)}) async-start(bf16[32,8,1024]{2,1,0:T(8,128)(2,1)} %stack.2), calls=%async_computation | async-start | bytes 1048576 | tf_op jit(solution)/shard_map/all_to_all | solution.py:33
  20.8 163.8 %all-reduce.5.cloned.1.call-start = ((), (), s32[]{:S(2)}) async-start(), calls=%async_computation.1 | async-start | bytes 1048576 | tf_op jit(solution)/shard_map/psum | solution.py:60
  37.1 3.6 copy-start.3
  42.2 302.0 %all-reduce.7.cloned.1.call-start = ((), (), s32[]{:S(2)}) async-start(), calls=%async_computation.2 | async-start | bytes 1048576 | tf_op jit(solution)/shard_map/psum | solution.py:60
  185.9 12.4 %collective-permute-start = (bf16[256,1024]{1,0:T(8,128)(2,1)S(1)}, bf16[256,1024]{1,0:T(8,128)(2,1)S(1)}, u32[]{:S(2)}, u32[]{:S(2)}) collective-permute-start(bf16[256,1024]{1,0:T(8,128)(2,1)S(1)} %fusion.18), channel_id=1, source_target_pairs={{224,0},{0,32},{32,64},{64,96},{96,128},{128,160},{160,192},{192,2... | collective-permute-start | bytes 1572872 | tf_op jit(solution)/shard_map/ppermute | solution.py:17
  195.3 5.1 copy-start.2
  202.0 302.0 %all-reduce.9.cloned.1.call-start = ((), (), s32[]{:S(2)}) async-start(), calls=%async_computation.3 | async-start | bytes 1048576 | tf_op jit(solution)/shard_map/psum | solution.py:60
  345.5 12.4 %collective-permute-start.1 = (bf16[256,1024]{1,0:T(8,128)(2,1)S(1)}, bf16[256,1024]{1,0:T(8,128)(2,1)S(1)}, u32[]{:S(2)}, u32[]{:S(2)}) collective-permute-start(bf16[256,1024]{1,0:T(8,128)(2,1)S(1)} %fusion.21), channel_id=1, source_target_pairs={{224,0},{0,32},{32,64},{64,96},{96,128},{128,160},{160,192},{192,2... | collective-permute-start | bytes 1572872 | tf_op jit(solution)/shard_map/ppermute | solution.py:17
  355.0 5.1 copy-start.1
  361.7 302.0 %all-reduce.11.cloned.1.call-start = ((), (), s32[]{:S(2)}) async-start(), calls=%async_computation.4 | async-start | bytes 1048576 | tf_op jit(solution)/shard_map/psum | solution.py:60
  505.3 12.4 %collective-permute-start.2 = (bf16[256,1024]{1,0:T(8,128)(2,1)S(1)}, bf16[256,1024]{1,0:T(8,128)(2,1)S(1)}, u32[]{:S(2)}, u32[]{:S(2)}) collective-permute-start(bf16[256,1024]{1,0:T(8,128)(2,1)S(1)} %fusion.24), channel_id=1, source_target_pairs={{224,0},{0,32},{32,64},{64,96},{96,128},{128,160},{160,192},{192,2... | collective-permute-start | bytes 1572872 | tf_op jit(solution)/shard_map/ppermute | solution.py:17
  514.7 5.1 copy-start
  664.9 12.4 %collective-permute-start.3 = (bf16[256,1024]{1,0:T(8,128)(2,1)S(1)}, bf16[256,1024]{1,0:T(8,128)(2,1)S(1)}, u32[]{:S(2)}, u32[]{:S(2)}) collective-permute-start(bf16[256,1024]{1,0:T(8,128)(2,1)S(1)} %fusion.27), channel_id=1, source_target_pairs={{224,0},{0,32},{32,64},{64,96},{96,128},{128,160},{160,192},{192,2... | collective-permute-start | bytes 1572872 | tf_op jit(solution)/shard_map/ppermute | solution.py:17
Sparse Core Ops, SparseCore 0:
  42.3 142.2 all-reduce.4
  202.2 142.0 all-reduce.6
  361.8 142.1 all-reduce.8
  521.5 142.0 all-reduce.10
